TPU v7x, 256 devices: a whole 4x4x8 slice. The times are simulated.
256 devices in a mesh: row: 32 (over z, y_lo, core), col: 8 (over x, y_hi).
Axes of the slice: x: 4, y: 4 (y_hi: 2, y_lo: 2; y = y_hi * 2 + y_lo), z: 8, core: 2. Of those that a mesh axis runs over, the one named last changes fastest.
Arguments:
- activations: bfloat16 [1024, 16384], P('col', 'row'), may hold values from -6 to 6
- out_grad: bfloat16 [1024, 16384], P('col', 'row'), may hold values from -2 to 2
- gate_pre: bfloat16 [1024, 8192], P('row', 'col'), may hold values from -6 to 6
- up_pre: bfloat16 [1024, 8192], P('row', 'col'), may hold values from -6 to 6
- gate_weight: bfloat16 [16384, 8192], P('row', 'col'), may hold values from -0.046875 to 0.046875
- up_weight: bfloat16 [16384, 8192], P('row', 'col'), may hold values from -0.046875 to 0.046875
- down_weight: bfloat16 [8192, 16384], P('col', 'row'), may hold values from -0.0625 to 0.0625
Outputs:
- input_grad: bfloat16 [1024, 16384], P('col', 'row')
- gate_grad: bfloat16 [16384, 8192], P('row', 'col')
- up_grad: bfloat16 [16384, 8192], P('row', 'col')
- down_grad: bfloat16 [8192, 16384], P('col', 'row')
All inputs are finite; a program needn't handle non-finite values.
Results may differ from a plain program's by a relative error of at most 0.0051.
Values may be sent and summed in bfloat16 or wider, within the bound.
A program may use at most 64 MiB of HBM per device.

v0:
```python
import jax
import jax.numpy as jnp
from jax import lax
from jax.sharding import PartitionSpec as P


def contract_rows(left, right):
    return lax.dot_general(
        left, right, (((0,), (0,)), ((), ())), preferred_element_type=jnp.float32
    )


def contract_cols(left, right):
    return lax.dot_general(
        left, right, (((1,), (1,)), ((), ())), preferred_element_type=jnp.float32
    )


def derive(hidden_grad, gate_pre, up_pre):
    gate_val = gate_pre.astype(jnp.float32)
    up_val = up_pre.astype(jnp.float32)
    gate_sig = jax.nn.sigmoid(gate_val)
    swish_val = gate_val * gate_sig
    hidden = (swish_val * up_val).astype(jnp.bfloat16)
    gate_back = (hidden_grad * up_val * gate_sig * (1.0 + gate_val * (1.0 - gate_sig))).astype(
        jnp.bfloat16
    )
    up_back = (hidden_grad * swish_val).astype(jnp.bfloat16)
    return (hidden, gate_back, up_back)


def per_device(activations, out_grad, gate_pre, up_pre, gate_weight, up_weight, down_weight):
    acts_all, grad_all = (
        lax.all_gather(activations, "col", axis=0, tiled=True),
        lax.all_gather(out_grad, "col", axis=0, tiled=True),
    )
    grad_rows = grad_all
    hidden_grad = lax.psum_scatter(
        contract_cols(grad_rows, down_weight), "row", scatter_dimension=0, tiled=True
    )
    hidden, gate_back, up_back = derive(hidden_grad, gate_pre, up_pre)
    hid_piece = lax.all_gather(hidden, "row", axis=0, tiled=True)
    gate_piece = lax.all_gather(gate_back, "row", axis=0, tiled=True)
    up_piece = lax.all_gather(up_back, "row", axis=0, tiled=True)
    grad_rows = grad_all
    down_acc = contract_rows(hid_piece, grad_rows)
    gate_acc = contract_rows(acts_all, gate_piece)
    up_acc = contract_rows(acts_all, up_piece)
    input_rows = contract_cols(gate_piece, gate_weight) + contract_cols(up_piece, up_weight)
    input_acc = input_rows
    down_acc, gate_acc, up_acc, input_acc = (down_acc, gate_acc, up_acc, input_acc)
    input_grad = lax.psum_scatter(input_acc, "col", scatter_dimension=0, tiled=True)
    return (
        input_grad.astype(jnp.bfloat16),
        gate_acc.astype(jnp.bfloat16),
        up_acc.astype(jnp.bfloat16),
        down_acc.astype(jnp.bfloat16),
    )


def solution(mesh):
    placed = (
        P("col", "row"),
        P("col", "row"),
        P("row", "col"),
        P("row", "col"),
        P("row", "col"),
        P("row", "col"),
        P("col", "row"),
    )
    return jax.shard_map(
        per_device,
        mesh=mesh,
        in_specs=placed,
        out_specs=(P("col", "row"), P("row", "col"), P("row", "col"), P("col", "row")),
        check_vma=False,
    )
```

profile of v0, /device:TPU:32, one launch (start us, length us, event | category | flops | bytes accessed | tf_op | source)
XLA Modules:
  0.0 538.8 jit_solution(6172015009212809988)
XLA Ops:
  7.2 0.0 copy-start
  7.2 0.0 all-gather.6.cloned.1.call-start
  7.2 0.7 all-gather.6.cloned.1.call-update
  7.9 0.0 reduce-scatter.3.cloned.1.call-start
  8.0 57.5 %all-gather.6.cloned.1.call-done = bf16[1024,512]{1,0:T(8,128)(2,1)} async-done(((bf16[128,512]{1,0:T(8,128)(2,1)}), bf16[1024,512]{1,0:T(8,128)(2,1)}) %all-gather.6.cloned.1.call-update) | async-done | bytes 1048592 | tf_op jit(solution)/shard_map/all_gather | solution.py:35
  65.5 0.0 copy-done
  65.5 4.4 fusion.10
  69.9 0.0 copy-start.1
  69.9 0.0 copy-start.2
  70.0 0.0 copy-start.3
  70.0 0.0 reduce-scatter.3.cloned.1.call-update
  70.0 0.0 all-gather.8.cloned.1.call-start
  70.0 117.0 %reduce-scatter.3.cloned.1.call-done = f32[32,1024]{1,0:T(8,128)} async-done(((f32[1024,1024]{1,0:T(8,128)}), f32[32,1024]{1,0:T(8,128)}) %reduce-scatter.3.cloned.1.call-update) | async-done | bytes 131088 | tf_op jit(solution)/shard_map/reduce_scatter | solution.py:38
  187.1 0.0 copy-done.1
  187.1 0.0 copy-done.2
  187.1 1.6 multiply_convert_fusion
  188.7 0.0 all-gather.8.cloned.1.call-update
  188.7 0.0 all-gather.10.cloned.1.call-start
  188.8 0.5 all-gather.10.cloned.1.call-update
  189.3 0.0 all-gather.12.cloned.1.call-start
  189.4 0.5 all-gather.12.cloned.1.call-update
  189.9 0.0 all-gather.14.cloned.1.call-start
  189.9 0.5 all-gather.14.cloned.1.call-update
  190.5 0.0 copy-start.4
  190.5 0.0 reduce-scatter.5.cloned.1.call-start
  190.5 67.7 %all-gather.8.cloned.1.call-done = bf16[1024,1024]{1,0:T(8,128)(2,1)} async-done(((bf16[32,1024]{1,0:T(8,128)(2,1)}), bf16[1024,1024]{1,0:T(8,128)(2,1)}) %all-gather.8.cloned.1.call-update) | async-done | bytes 2097168 | tf_op jit(solution)/shard_map/all_gather | solution.py:43
  258.2 0.0 copy-done.3
  258.2 4.2 fusion.11
  262.5 62.1 %all-gather.10.cloned.1.call-done = bf16[1024,1024]{1,0:T(8,128)(2,1)} async-done(((bf16[32,1024]{1,0:T(8,128)(2,1)}), bf16[1024,1024]{1,0:T(8,128)(2,1)}) %all-gather.10.cloned.1.call-update) | async-done | bytes 2097168 | tf_op jit(solution)/shard_map/all_gather | solution.py:44
  324.5 0.0 copy-done.4
  324.5 4.9 convolution_add_fusion
  329.4 0.0 reduce-scatter.5.cloned.1.call-update
  329.5 50.4 %all-gather.12.cloned.1.call-done = bf16[1024,512]{1,0:T(8,128)(2,1)} async-done(((bf16[128,512]{1,0:T(8,128)(2,1)}), bf16[1024,512]{1,0:T(8,128)(2,1)}) %all-gather.12.cloned.1.call-update) | async-done | bytes 1048592 | tf_op jit(solution)/shard_map/all_gather | solution.py:34
  379.9 3.1 fusion
  383.0 0.0 copy-start.6
  383.0 1.3 copy.11
  384.3 0.0 copy-done.6
  384.3 2.9 fusion.1
  387.2 0.0 copy-start.5
  387.2 1.3 copy.12
  388.6 55.5 %all-gather.14.cloned.1.call-done = bf16[1024,1024]{1,0:T(8,128)(2,1)} async-done(((bf16[32,1024]{1,0:T(8,128)(2,1)}), bf16[1024,1024]{1,0:T(8,128)(2,1)}) %all-gather.14.cloned.1.call-update) | async-done | bytes 2097168 | tf_op jit(solution)/shard_map/all_gather | solution.py:42
  444.0 0.0 copy-done.5
  444.0 3.8 convolution_convert_fusion
  447.9 82.5 %reduce-scatter.5.cloned.1.call-done = f32[128,512]{1,0:T(8,128)} async-done(((f32[1024,512]{1,0:T(8,128)}), f32[128,512]{1,0:T(8,128)}) %reduce-scatter.5.cloned.1.call-update) | async-done | bytes 262160 | tf_op jit(solution)/shard_map/reduce_scatter | solution.py:52
  530.4 1.6 convert_element_type.37
Async XLA Ops:
  7.2 58.3 %copy-start = (bf16[1024,512]{1,0:T(8,128)(2,1)S(1)}, bf16[1024,512]{1,0:T(8,128)(2,1)}, u32[]{:S(2)}) copy-start(bf16[1024,512]{1,0:T(8,128)(2,1)} %param.13) | copy-start | bytes 3145732
  7.2 58.3 %all-gather.6.cloned.1.call-start = ((), (), s32[]{:S(2)}) async-start(), calls=%async_computation.2 | async-start | bytes 1179648 | tf_op jit(solution)/shard_map/all_gather | solution.py:35
  7.9 179.1 %reduce-scatter.3.cloned.1.call-start = ((), (), s32[]{:S(2)}) async-start(), calls=%async_computation.3 | async-start | bytes 4325376 | tf_op jit(solution)/shard_map/reduce_scatter | solution.py:38
  69.9 117.1 %copy-start.1 = (bf16[32,1024]{1,0:T(8,128)(2,1)S(1)}, bf16[32,1024]{1,0:T(8,128)(2,1)}, u32[]{:S(2)}) copy-start(bf16[32,1024]{1,0:T(8,128)(2,1)} %param.9) | copy-start | bytes 196612
  69.9 117.1 %copy-start.2 = (bf16[32,1024]{1,0:T(8,128)(2,1)S(1)}, bf16[32,1024]{1,0:T(8,128)(2,1)}, u32[]{:S(2)}) copy-start(bf16[32,1024]{1,0:T(8,128)(2,1)} %param.10) | copy-start | bytes 196612
  70.0 188.3 %copy-start.3 = (bf16[512,1024]{1,0:T(8,128)(2,1)S(1)}, bf16[512,1024]{1,0:T(8,128)(2,1)}, u32[]{:S(2)}) copy-start(bf16[512,1024]{1,0:T(8,128)(2,1)} %param.11) | copy-start | bytes 3145732
  70.0 188.2 %all-gather.8.cloned.1.call-start = ((), (), s32[]{:S(2)}) async-start(), calls=%async_computation.4 | async-start | bytes 2162688 | tf_op jit(solution)/shard_map/all_gather | solution.py:43
  188.7 135.8 %all-gather.10.cloned.1.call-start = ((), (), s32[]{:S(2)}) async-start(), calls=%async_computation.5 | async-start | bytes 2162688 | tf_op jit(solution)/shard_map/all_gather | solution.py:44
  189.3 190.6 %all-gather.12.cloned.1.call-start = ((), (), s32[]{:S(2)}) async-start(), calls=%async_computation.7 | async-start | bytes 1179648 | tf_op jit(solution)/shard_map/all_gather | solution.py:34
  189.9 254.2 %all-gather.14.cloned.1.call-start = ((), (), s32[]{:S(2)}) async-start(), calls=%async_computation.8 | async-start | bytes 2162688 | tf_op jit(solution)/shard_map/all_gather | solution.py:42
  190.5 134.1 %copy-start.4 = (bf16[512,1024]{1,0:T(8,128)(2,1)S(1)}, bf16[512,1024]{1,0:T(8,128)(2,1)}, u32[]{:S(2)}) copy-start(bf16[512,1024]{1,0:T(8,128)(2,1)} %param.12) | copy-start | bytes 3145732
  190.5 339.9 %reduce-scatter.5.cloned.1.call-start = ((), (), s32[]{:S(2)}) async-start(), calls=%async_computation.6 | async-start | bytes 2359296 | tf_op jit(solution)/shard_map/reduce_scatter | solution.py:52
  383.0 1.3 copy-start.6
  387.2 56.8 %copy-start.5 = (bf16[1024,512]{1,0:T(8,128)(2,1)S(1)}, bf16[1024,512]{1,0:T(8,128)(2,1)}, u32[]{:S(2)}) copy-start(bf16[1024,512]{1,0:T(8,128)(2,1)} %all-gather.6.cloned.1.call-done) | copy-start | bytes 3145732
Sparse Core Ops, SparseCore 0:
  10.6 54.8 all-gather.5
  70.1 116.9 reduce-scatter.2
  189.5 68.6 all-gather.7
  260.5 63.9 all-gather.9
  327.0 52.8 all-gather.11
  381.6 62.4 all-gather.13
  448.1 82.2 reduce-scatter.4
where the time goes:
time: 539 us
  waiting for transfers between devices  495 us (92%)
  matrix products  23.4 us (4%)
  between operations  14.2 us (3%)
    reduce_scatter x1, waiting for transfers between devices, per_device(): lax.psum_scatter(contract_cols(grad_rows, down_weight), 'row', scatter_di...  117 us
    reduce_scatter x1, waiting for transfers between devices, per_device(): lax.psum_scatter(input_acc, 'col', scatter_dimension=0, tiled=True)  82.5 us
    all_gather x1, waiting for transfers between devices, per_device(): gate_piece = lax.all_gather(gate_back, 'row', axis=0, tiled=True)  67.7 us
    all_gather x1, waiting for transfers between devices, per_device(): up_piece = lax.all_gather(up_back, 'row', axis=0, tiled=True)  62.1 us
    all_gather x1, waiting for transfers between devices, per_device(): lax.all_gather(out_grad, 'col', axis=0, tiled=True)  57.5 us
    all_gather x1, waiting for transfers between devices, per_device(): hid_piece = lax.all_gather(hidden, 'row', axis=0, tiled=True)  55.5 us
    all_gather x1, waiting for transfers between devices, per_device(): lax.all_gather(activations, 'col', axis=0, tiled=True)  50.4 us
    dot_general x3, matrix products, contract_cols(): lax.dot_general(left, right, (((1,), (1,)), ((), ())), preferred_element_...  13.6 us
  transfers between devices with their start and end apart: 7, of which 7 were waited for; matrix products, arithmetic and copies ran while one was open for 4% of the time, Pallas kernels for 0%

commit v1 on v0

--- a/solution.py
+++ b/solution.py
@@ -39,8 +39,12 @@
         contract_cols(grad_rows, down_weight), "row", scatter_dimension=0, tiled=True
     )
     hidden, gate_back, up_back = derive(hidden_grad, gate_pre, up_pre)
-    hid_piece = lax.all_gather(hidden, "row", axis=0, tiled=True)
-    gate_piece = lax.all_gather(gate_back, "row", axis=0, tiled=True)
+    link_the_block = lambda buf, xx: jnp.split(
+        jax.lax.all_gather(jnp.concatenate([buf, xx], axis=1), "row", tiled=True, axis=0),
+        [buf.shape[1]],
+        axis=1,
+    )
+    hid_piece, gate_piece = link_the_block(hidden, gate_back)
     up_piece = lax.all_gather(up_back, "row", axis=0, tiled=True)
     grad_rows = grad_all
     down_acc = contract_rows(hid_piece, grad_rows)

time: 539 us -> 476 us (0.88)
  waiting for transfers between devices: 495 us -> 431 us
    all_gather x2 -> x1, waiting for transfers between devices: 123 us -> 64.3 us  [per_device(): jax.lax.all_gather(jnp.concatenate([buf, xx], axis=1), 'row', tiled=True,...]
    reduce_scatter x1, waiting for transfers between devices: 82.5 us -> 71.8 us  [per_device(): lax.psum_scatter(input_acc, 'col', scatter_dimension=0, tiled=True)]
    all_gather x1, waiting for transfers between devices: 62.1 us -> 67.9 us  [per_device(): up_piece = lax.all_gather(up_back, 'row', axis=0, tiled=True)]
  transfers between devices with their start and end apart: 7 -> 6, of which waited for: 7 -> 6; matrix products, arithmetic and copies ran while one was open for 4% -> 5% of each run, Pallas kernels for 0% -> 0%
where the time goes in v1:
time: 476 us; the launch traced here: 475 us
  waiting for transfers between devices  431 us (91%)
  matrix products  23.8 us (5%)
  between operations  14.1 us (3%)
    reduce_scatter x1, waiting for transfers between devices, per_device(): lax.psum_scatter(contract_cols(grad_rows, down_weight), 'row', scatter_di...  117 us
    reduce_scatter x1, waiting for transfers between devices, per_device(): lax.psum_scatter(input_acc, 'col', scatter_dimension=0, tiled=True)  71.8 us
    all_gather x1, waiting for transfers between devices, per_device(): up_piece = lax.all_gather(up_back, 'row', axis=0, tiled=True)  67.9 us
    all_gather x1, waiting for transfers between devices, per_device(): jax.lax.all_gather(jnp.concatenate([buf, xx], axis=1), 'row', tiled=True,...  64.3 us
    all_gather x1, waiting for transfers between devices, per_device(): lax.all_gather(out_grad, 'col', axis=0, tiled=True)  57.5 us
    all_gather x1, waiting for transfers between devices, per_device(): lax.all_gather(activations, 'col', axis=0, tiled=True)  50.7 us
    dot_general x3, matrix products, contract_cols(): lax.dot_general(left, right, (((1,), (1,)), ((), ())), preferred_element_...  13.6 us
    dot_general x3, matrix products, contract_rows(): lax.dot_general(left, right, (((0,), (0,)), ((), ())), preferred_element_...  10.2 us
  transfers between devices with their start and end apart: 6, of which 6 were waited for; matrix products, arithmetic and copies ran while one was open for 5% of the time, Pallas kernels for 0%

profile of v1, /device:TPU:32, one launch (start us, length us, event | category | flops | bytes accessed | tf_op | source)
XLA Modules:
  0.0 475.3 jit_solution(4923595145288498146)
XLA Ops:
  7.2 0.0 copy-start
  7.2 0.0 all-gather.5.cloned.1.call-start
  7.2 0.7 all-gather.5.cloned.1.call-update
  7.9 0.0 reduce-scatter.3.cloned.1.call-start
  8.0 57.5 %all-gather.5.cloned.1.call-done = bf16[1024,512]{1,0:T(8,128)(2,1)} async-done(((bf16[128,512]{1,0:T(8,128)(2,1)}), bf16[1024,512]{1,0:T(8,128)(2,1)}) %all-gather.5.cloned.1.call-update) | async-done | bytes 1048592 | tf_op jit(solution)/shard_map/all_gather | solution.py:35
  65.5 0.0 copy-done
  65.5 4.5 fusion.27
  70.0 0.0 copy-start.1
  70.0 0.0 copy-start.2
  70.0 0.0 copy-start.3
  70.0 0.0 reduce-scatter.3.cloned.1.call-update
  70.0 0.0 all-gather.9.cloned.1.call-start
  70.1 117.1 %reduce-scatter.3.cloned.1.call-done = f32[32,1024]{1,0:T(8,128)} async-done(((f32[1024,1024]{1,0:T(8,128)}), f32[32,1024]{1,0:T(8,128)}) %reduce-scatter.3.cloned.1.call-update) | async-done | bytes 131088 | tf_op jit(solution)/shard_map/reduce_scatter | solution.py:38
  187.1 0.0 copy-done.1
  187.1 0.0 copy-done.2
  187.1 1.6 fusion.22
  188.7 0.0 all-gather.9.cloned.1.call-update
  188.8 0.0 all-gather.7.cloned.1.call-start
  188.8 0.7 pad_maximum_fusion
  189.5 0.0 all-gather.7.cloned.1.call-update
  189.5 0.0 all-gather.11.cloned.1.call-start
  189.5 0.5 all-gather.11.cloned.1.call-update
  190.1 0.0 copy-start.4
  190.1 0.0 reduce-scatter.5.cloned.1.call-start
  190.1 67.9 %all-gather.9.cloned.1.call-done = bf16[1024,1024]{1,0:T(8,128)(2,1)} async-done(((bf16[32,1024]{1,0:T(8,128)(2,1)}), bf16[1024,1024]{1,0:T(8,128)(2,1)}) %all-gather.9.cloned.1.call-update) | async-done | bytes 2097168 | tf_op jit(solution)/shard_map/all_gather | solution.py:48
  258.1 0.0 copy-done.3
  258.1 4.2 fusion.28
  262.3 64.3 %all-gather.7.cloned.1.call-done = bf16[1024,2048]{1,0:T(8,128)(2,1)} async-done(((bf16[32,2048]{1,0:T(8,128)(2,1)}), bf16[1024,2048]{1,0:T(8,128)(2,1)}) %all-gather.7.cloned.1.call-update) | async-done | bytes 4194320 | tf_op jit(solution)/shard_map/all_gather | solution.py:43
  326.6 0.0 copy-done.4
  326.6 4.9 %fusion.6 = f32[1024,512]{1,0:T(8,128)} fusion(f32[1024,512]{1,0:T(8,128)} %fusion.28, bf16[512,1024]{1,0:T(8,128)(2,1)S(1)} %copy-done.4, bf16[1024,2048]{1,0:T(8,128)(2,1)} %all-gather.7.cloned.1.call-done), kind=kOutput, calls=%fused_computation.6 | convolution fusion | flops 1074266112 | bytes 7340032 | tf_op jit(solution)/shard_map/dot_general | solution.py:14
  331.5 0.0 reduce-scatter.5.cloned.1.call-update
  331.5 50.7 %all-gather.11.cloned.1.call-done = bf16[1024,512]{1,0:T(8,128)(2,1)} async-done(((bf16[128,512]{1,0:T(8,128)(2,1)}), bf16[1024,512]{1,0:T(8,128)(2,1)}) %all-gather.11.cloned.1.call-update) | async-done | bytes 1048592 | tf_op jit(solution)/shard_map/all_gather | solution.py:34
  382.2 3.1 fusion.15
  385.3 1.3 copy.12
  386.6 0.0 copy-start.5
  386.6 3.2 fusion.16
  389.9 1.3 copy.11
  391.2 0.0 copy-done.5
  391.2 3.8 fusion.12
  395.0 71.8 %reduce-scatter.5.cloned.1.call-done = f32[128,512]{1,0:T(8,128)} async-done(((f32[1024,512]{1,0:T(8,128)}), f32[128,512]{1,0:T(8,128)}) %reduce-scatter.5.cloned.1.call-update) | async-done | bytes 262160 | tf_op jit(solution)/shard_map/reduce_scatter | solution.py:56
  466.8 1.6 convert_element_type.38
Async XLA Ops:
  7.2 58.3 %copy-start = (bf16[1024,512]{1,0:T(8,128)(2,1)S(1)}, bf16[1024,512]{1,0:T(8,128)(2,1)}, u32[]{:S(2)}) copy-start(bf16[1024,512]{1,0:T(8,128)(2,1)} %param.13) | copy-start | bytes 3145732
  7.2 58.3 %all-gather.5.cloned.1.call-start = ((), (), s32[]{:S(2)}) async-start(), calls=%async_computation.2 | async-start | bytes 1179648 | tf_op jit(solution)/shard_map/all_gather | solution.py:35
  7.9 179.2 %reduce-scatter.3.cloned.1.call-start = ((), (), s32[]{:S(2)}) async-start(), calls=%async_computation.3 | async-start | bytes 4325376 | tf_op jit(solution)/shard_map/reduce_scatter | solution.py:38
  70.0 117.1 %copy-start.1 = (bf16[32,1024]{1,0:T(8,128)(2,1)S(1)}, bf16[32,1024]{1,0:T(8,128)(2,1)}, u32[]{:S(2)}) copy-start(bf16[32,1024]{1,0:T(8,128)(2,1)} %param.10) | copy-start | bytes 196612
  70.0 117.1 %copy-start.2 = (bf16[32,1024]{1,0:T(8,128)(2,1)S(1)}, bf16[32,1024]{1,0:T(8,128)(2,1)}, u32[]{:S(2)}) copy-start(bf16[32,1024]{1,0:T(8,128)(2,1)} %param.9) | copy-start | bytes 196612
  70.0 188.1 %copy-start.3 = (bf16[512,1024]{1,0:T(8,128)(2,1)S(1)}, bf16[512,1024]{1,0:T(8,128)(2,1)}, u32[]{:S(2)}) copy-start(bf16[512,1024]{1,0:T(8,128)(2,1)} %param.12) | copy-start | bytes 3145732
  70.0 188.1 %all-gather.9.cloned.1.call-start = ((), (), s32[]{:S(2)}) async-start(), calls=%async_computation.5 | async-start | bytes 2162688 | tf_op jit(solution)/shard_map/all_gather | solution.py:48
  188.8 137.8 %all-gather.7.cloned.1.call-start = ((), (), s32[]{:S(2)}) async-start(), calls=%async_computation.4 | async-start | bytes 4325376 | tf_op jit(solution)/shard_map/all_gather | solution.py:43
  189.5 192.7 %all-gather.11.cloned.1.call-start = ((), (), s32[]{:S(2)}) async-start(), calls=%async_computation.7 | async-start | bytes 1179648 | tf_op jit(solution)/shard_map/all_gather | solution.py:34
  190.1 136.5 %copy-start.4 = (bf16[512,1024]{1,0:T(8,128)(2,1)S(1)}, bf16[512,1024]{1,0:T(8,128)(2,1)}, u32[]{:S(2)}) copy-start(bf16[512,1024]{1,0:T(8,128)(2,1)} %param.11) | copy-start | bytes 3145732
  190.1 276.7 %reduce-scatter.5.cloned.1.call-start = ((), (), s32[]{:S(2)}) async-start(), calls=%async_computation.6 | async-start | bytes 2359296 | tf_op jit(solution)/shard_map/reduce_scatter | solution.py:56
  386.6 4.5 copy-start.5
Sparse Core Ops, SparseCore 0:
  10.6 54.8 all-gather.4
  70.1 116.9 reduce-scatter.2
  189.5 68.4 all-gather.8
  260.4 66.1 all-gather.6
  329.1 53.0 all-gather.10
  386.1 80.6 reduce-scatter.4
